TPU v7x, 256 devices: a whole 4x4x8 slice. The times are simulated.
256 devices in a mesh: grp: 32 (over y, z), head: 8 (over x, core).
Axes of the slice: x: 4, y: 4, z: 8, core: 2. Of those that a mesh axis runs over, the one named last changes fastest.
Arguments:
- tokens: bfloat16 [16384, 1024], P(('grp', 'head')), may hold values from -6 to 6
- norm_gain: float32 [1024], replicated, may hold values from 0.5 to 1.5
- w_qkv: bfloat16 [1024, 3072], replicated, may hold values from -0.1875 to 0.1875
- w_gates: bfloat16 [1024, 16], replicated, may hold values from -0.1875 to 0.1875
- conv_weight: float32 [4, 3072], replicated, may hold values from -3 to 3
- conv_state: bfloat16 [32, 3, 3072], P('grp'), may hold values from -6 to 6
- decay_rate: float32 [8], replicated, may hold values from 0.0005 to 0.1
- ridge: float32 [8], P('head'), may hold values from 0.25 to 2
- w_out: bfloat16 [1024, 1024], replicated, may hold values from -0.1875 to 0.1875
- cache_keys: bfloat16 [2048, 128, 8, 128], P('grp', None, 'head'), may hold values from -0.59765625 to 0.59765625
- cache_values: bfloat16 [2048, 128, 8, 128], P('grp', None, 'head'), may hold values from -6 to 6
- page_table: int32 [32, 64], replicated, may hold values from 0 to 2047, as said below
- cache_lengths: int32 [32], replicated, may hold values from 1 to 8192, 131072 in all
- group_prompt: int32 [32], replicated, may hold values from 0 to 31
- prompt_state: float32 [32, 8, 2, 128, 128], P('grp', 'head'), may hold values from -8 to 16
Outputs:
- layer_out: bfloat16 [16384, 1024], P(('grp', 'head'))
Inputs may be any that keep to these rules, and one draw needn't show every extreme that they name: `page_table`: every pool page is named exactly once in the table; each pool shard of 64 consecutive pages holds exactly 2 pages of every group's requests. `cache_lengths`: some request has exactly 8192 cached tokens.
All inputs are finite; a program needn't handle non-finite values.
Results may differ from a plain program's by a relative error of at most 0.0045.
Values may be sent and summed in bfloat16 or wider, within the bound.
A program may use at most 128 MiB of HBM per device.

v0:
```python
import jax
import jax.numpy as jnp
from jax import lax
from jax.sharding import PartitionSpec as P

HEADS = 8
HDIM = 128
CONV = 4
NEW = 512
CG_STEPS = 8
PAGE = 128
REQ_GRP = 1
PAGES_MAX = 64
POOL_DEV = 64


PRECISE = lax.Precision.HIGHEST
EPS_NORM = 1e-06


def from_behind(block, axis, distance):
    devices = range(lax.axis_size(axis))
    route = [(i - distance, i) for i in devices if i - distance in devices]
    return lax.ppermute(block, axis, route)


def unit_rows(block):
    return block * lax.rsqrt(jnp.sum(block * block, axis=-1, keepdims=True) + EPS_NORM)


def ridge_read(
    query, key_rows, value_rows, write_gate, log_gamma, start_gram, start_cross, ridge_add, steps
):
    length = query.shape[2]
    positions = jnp.arange(length)
    causal = positions[:, None] >= positions[None, :]
    lower_tri = causal.astype(jnp.float32)
    cumul = jnp.einsum("ts,rhs->rht", lower_tri, log_gamma, precision=PRECISE)
    spread = jnp.where(causal, cumul[..., :, None] - cumul[..., None, :], -jnp.inf)
    weights = jnp.exp(spread) * write_gate[..., None, :]
    carry_scale = jnp.exp(cumul)[..., None]
    ridge_term = ridge_add[None, :, None, None]
    solved = jnp.zeros_like(query)
    residue = query
    direction = query
    norm_now = jnp.sum(residue * residue, axis=-1, keepdims=True)
    for cg_step in range(steps):
        apply_from_start = jnp.einsum("rhte,rhfe->rhtf", direction, start_gram, precision=PRECISE)
        apply_scores = (
            jnp.einsum("rhte,rhse->rhts", direction, key_rows, precision=PRECISE) * weights
        )
        image = (
            carry_scale * apply_from_start
            + ridge_term * direction
            + jnp.einsum("rhts,rhse->rhte", apply_scores, key_rows, precision=PRECISE)
        )
        alpha = norm_now / jnp.sum(direction * image, axis=-1, keepdims=True)
        solved = solved + alpha * direction
        residue = residue - alpha * image
        norm_next = jnp.sum(residue * residue, axis=-1, keepdims=True)
        direction = residue + norm_next / norm_now * direction
        norm_now = norm_next
    from_start = carry_scale * jnp.einsum("rhte,rhfe->rhtf", solved, start_cross, precision=PRECISE)
    scores = jnp.einsum("rhte,rhse->rhts", solved, key_rows, precision=PRECISE) * weights
    return from_start + jnp.einsum("rhts,rhsf->rhtf", scores, value_rows, precision=PRECISE)


def page_sums(keys_live, values_all):
    page_grams = jnp.einsum(
        "pthe,pthf->phef", keys_live, keys_live, preferred_element_type=jnp.float32
    )
    page_cross = jnp.einsum(
        "pthf,pthe->phfe", values_all, keys_live, preferred_element_type=jnp.float32
    )
    return jnp.stack([page_grams, page_cross], axis=2).reshape(keys_live.shape[0], -1)


def shards(
    tokens,
    norm_gain,
    w_qkv,
    w_gates,
    conv_weight,
    conv_state,
    decay_rate,
    ridge,
    w_out,
    cache_keys,
    cache_values,
    page_table,
    cache_lengths,
    group_prompt,
    prompt_state,
):
    tok_rows = tokens.shape[0]
    head_count = lax.axis_size("head")
    heads_here = HEADS // head_count
    group_rows = tok_rows * head_count
    widened = tokens.astype(jnp.float32)
    normed = (
        widened
        * lax.rsqrt(jnp.mean(widened * widened, axis=-1, keepdims=True) + EPS_NORM)
        * norm_gain
    ).astype(jnp.bfloat16)
    mixed_in = jnp.dot(normed, w_qkv, preferred_element_type=jnp.float32).astype(jnp.bfloat16)
    mixed_in = lax.optimization_barrier(mixed_in)
    gate_logits = jnp.dot(normed, w_gates, preferred_element_type=jnp.float32).reshape(
        tok_rows, HEADS, 2
    )
    write_gate = jax.nn.sigmoid(gate_logits[..., 0]).astype(jnp.bfloat16)
    log_gamma = (-decay_rate * jax.nn.softplus(gate_logits[..., 1])).astype(jnp.bfloat16)
    tail_rows = from_behind(mixed_in[tok_rows - (CONV - 1) :], "head", 1)
    extended = jnp.concatenate([tail_rows, mixed_in], axis=0).astype(jnp.float32)
    local_pos = lax.axis_index("head") * tok_rows + jnp.arange(tok_rows)
    in_request = local_pos % NEW
    request_here = local_pos // NEW
    state_rows = conv_state.reshape(-1, conv_state.shape[-1]).astype(jnp.float32)
    state_slots = jnp.arange(state_rows.shape[0])
    conv_sum = conv_weight[CONV - 1] * extended[CONV - 1 :]
    for lag_step in range(1, CONV):
        earlier = extended[CONV - 1 - lag_step : CONV - 1 - lag_step + tok_rows]
        picked = request_here * (CONV - 1) + jnp.clip(CONV - 1 + in_request - lag_step, 0, CONV - 2)
        one_hot = (picked[:, None] == state_slots[None, :]).astype(jnp.float32)
        stored = jnp.dot(one_hot, state_rows, precision=PRECISE)
        earlier = jnp.where((in_request >= lag_step)[:, None], earlier, stored)
        conv_sum = conv_sum + conv_weight[CONV - 1 - lag_step] * earlier
    conv_sum = conv_sum.reshape(tok_rows, HEADS, 3, HDIM)
    query = unit_rows(jax.nn.silu(conv_sum[:, :, 0]))
    key_vec = unit_rows(jax.nn.silu(conv_sum[:, :, 1]))
    value_vec = conv_sum[:, :, 2]
    stacked = jnp.stack([query, key_vec, value_vec], axis=2).astype(jnp.bfloat16)
    stacked = stacked.reshape(tok_rows, head_count, heads_here * 3 * HDIM)
    gate_pair = jnp.stack([write_gate, log_gamma], axis=-1)
    head_rows, head_gates = (
        lax.all_to_all(stacked, "head", split_axis=1, concat_axis=0, tiled=True),
        lax.all_to_all(gate_pair, "head", split_axis=1, concat_axis=0, tiled=True),
    )
    grp_index = lax.axis_index("grp")
    local_ids = grp_index * POOL_DEV + jnp.arange(POOL_DEV)
    page_match = page_table[:, :, None] == local_ids[None, None, :]
    live_count = jnp.clip(cache_lengths[:, None] - jnp.arange(PAGES_MAX)[None, :] * PAGE, 0, PAGE)
    page_live = jnp.sum(jnp.where(page_match, live_count[:, :, None], 0), axis=(0, 1))
    token_mask = (jnp.arange(PAGE)[None, :] < page_live[:, None]).astype(jnp.bfloat16)
    keys_live = cache_keys * token_mask[:, :, None, None]
    prompt_flat = prompt_state.reshape(1, -1)
    owner_map = jnp.any(page_match, axis=1).astype(jnp.float32)
    per_page = page_sums(keys_live, cache_values)
    term_rows = jnp.dot(owner_map, per_page, precision=PRECISE, preferred_element_type=jnp.float32)
    gram_rows = lax.psum_scatter(
        term_rows.astype(jnp.bfloat16), "grp", scatter_dimension=0, tiled=True
    ).astype(jnp.float32)
    my_prompt = group_prompt[grp_index]
    shard_piece = lax.all_gather(
        prompt_state.astype(jnp.bfloat16), "grp", axis=0, tiled=True
    ).astype(jnp.float32)
    hit_mask = (jnp.arange(shard_piece.shape[0]) == my_prompt).astype(jnp.float32)
    chosen = jnp.zeros((prompt_flat.shape[1],), jnp.float32) + jnp.sum(
        hit_mask[:, None] * shard_piece.reshape(shard_piece.shape[0], -1), axis=0
    )
    gram_rows = gram_rows + chosen[None, :]
    start_state = gram_rows.reshape(REQ_GRP, heads_here, 2, HDIM, HDIM)
    head_rows = head_rows.reshape(REQ_GRP, NEW, heads_here, 3, HDIM).astype(jnp.float32)
    head_rows = jnp.transpose(head_rows, (0, 2, 1, 3, 4))
    head_gates = head_gates.reshape(REQ_GRP, NEW, heads_here, 2).astype(jnp.float32)
    head_gates = jnp.transpose(head_gates, (0, 2, 1, 3))
    read_out = ridge_read(
        head_rows[:, :, :, 0],
        head_rows[:, :, :, 1],
        head_rows[:, :, :, 2],
        head_gates[..., 0],
        head_gates[..., 1],
        start_state[:, :, 0],
        start_state[:, :, 1],
        ridge,
        CG_STEPS,
    )
    read_out = jnp.transpose(read_out.astype(jnp.bfloat16), (0, 2, 1, 3)).reshape(
        group_rows, heads_here * HDIM
    )
    returned = lax.all_to_all(
        read_out.reshape(group_rows, 1, heads_here * HDIM),
        "head",
        split_axis=0,
        concat_axis=1,
        tiled=True,
    )
    attended = jnp.dot(
        returned.reshape(tok_rows, HEADS * HDIM), w_out, preferred_element_type=jnp.float32
    )
    return (widened + attended).astype(jnp.bfloat16)


def solution(mesh):
    placed = (
        P(("grp", "head"), None),
        P(),
        P(),
        P(),
        P(),
        P("grp", None, None),
        P(),
        P("head"),
        P(),
        P("grp", None, "head", None),
        P("grp", None, "head", None),
        P(),
        P(),
        P(),
        P("grp", "head", None, None, None),
    )
    return jax.shard_map(
        shards, mesh=mesh, in_specs=placed, out_specs=P(("grp", "head"), None), check_vma=False
    )
```

profile of v0, /device:TPU:1, one launch (start us, length us, event | category | flops | bytes accessed | tf_op | source)
XLA Modules:
  0.0 286.7 jit_solution(10611423669174919676)
XLA Ops:
  6.5 1.7 convert_element_type.95
  8.3 1.0 fusion.52
  9.4 4.2 %convolution_convert_fusion.1 = bf16[64,3072]{1,0:T(8,128)(2,1)S(1)} fusion(bf16[1024,3072]{1,0:T(8,128)(2,1)} %param.17, bf16[64,1024]{1,0:T(8,128)(2,1)} %param.15, f32[1024]{0:T(1024)} %param.16, f32[64]{0:T(128)S(1)} %add_rsqrt_fusion.2), kind=kOutput, calls=%fused_computation.3 | convolution fusion | flops 403111936 | bytes 6820096 | tf_op jit(solution)/shard_map/dot_general | solution.py:105
  13.6 4.5 %collective-permute-start = (bf16[3,3072]{1,0:T(4,128)(2,1)S(1)}, bf16[3,3072]{1,0:T(4,128)(2,1)S(1)}, u32[]{:S(2)}, u32[]{:S(2)}) collective-permute-start(bf16[3,3072]{1,0:T(4,128)(2,1)S(1)} %slice.93), channel_id=1, source_target_pairs={{0,1},{1,2},{2,3},{3,4},{4,5},{5,6},{6,7},{8,9},{9,10},{10,11},{11... | collective-permute-start | bytes 55304 | tf_op jit(solution)/shard_map/ppermute | solution.py:24
  18.5 0.6 copy.113
  19.1 4.1 %all-to-all-start = ((bf16[64,8,2]{0,2,1:T(2,128)(2,1)}), bf16[64,8,2]{0,2,1:T(2,128)(2,1)S(1)}, u32[]{:S(2)}, u32[]{:S(2)}) async-start(bf16[64,8,2]{0,2,1:T(2,128)(2,1)} %copy.113), calls=%async_computation | async-start | bytes 8192 | tf_op jit(solution)/shard_map/all_to_all | solution.py:136
  23.3 0.7 fusion.27
  24.1 5.5 %convolution_bitcast_fusion.1 = f32[64,1,1,128,128]{4,3,0,2,1:T(8,128)S(1)} fusion(bf16[64,128,1,128]{3,1,2,0:T(8,128)(2,1)} %param.24, bf16[64,128]{1,0:T(8,128)(2,1)S(1)} %fusion.102), kind=kOutput, calls=%fused_computation.5 | convolution fusion | flops 269484032 | bytes 6307840 | tf_op jit(solution)/shard_map/pthe,pthf->phef/dot_general | solution.py:69
  29.6 2.6 convolution_bitcast_fusion
  32.2 1.1 pad_maximum_fusion
  33.3 3.8 %copy.126 = f32[64,1,2,128,128]{4,3,2,0,1:T(8,128)} copy(f32[64,1,2,128,128]{4,3,0,2,1:T(8,128)S(1)} %pad_maximum_fusion) | data formatting | bytes 16777216 | tf_op jit(solution)/shard_map/stack | solution.py:75
  37.1 9.4 %reshape.724 = f32[64,32768]{1,0:T(8,128)} reshape(f32[64,1,2,128,128]{4,3,2,0,1:T(8,128)} %copy.126) | data formatting | bytes 16777216 | tf_op jit(solution)/shard_map/reshape | solution.py:75
  46.9 8.2 %convolution_convert_fusion = bf16[32,32768]{1,0:T(8,128)(2,1)} fusion(pred[32,64]{1,0:T(8,128)(4,1)S(1)} %compare_reduce_fusion, f32[64,32768]{1,0:T(8,128)} %reshape.724), kind=kOutput, calls=%fused_computation | convolution fusion | flops 806354944 | bytes 10487808 | tf_op jit(solution)/shard_map/dot_general | solution.py:148
  55.2 0.6 copy-done.4
  56.2 1.2 fusion.101
  57.4 0.7 dynamic_slice.3
  58.1 0.7 compare_convert_fusion
  59.4 0.6 dynamic-slice
  60.2 1.7 fusion.32
  61.9 0.6 reshape.719
  64.0 0.8 copy.121
  64.8 4.8 %all-to-all-start.1 = ((bf16[64,8,384]{2,0,1:T(8,128)(2,1)}), bf16[64,8,384]{2,0,1:T(8,128)(2,1)S(1)}, u32[]{:S(2)}, u32[]{:S(2)}) async-start(bf16[64,8,384]{2,0,1:T(8,128)(2,1)} %copy.121), calls=%async_computation.1 | async-start | bytes 786432 | tf_op jit(solution)/shard_map/all_to_all | solution.py:135
  69.9 7.5 %all-to-all-done.1 = bf16[64,8,384]{2,0,1:T(8,128)(2,1)S(1)} async-done(((bf16[64,8,384]{2,0,1:T(8,128)(2,1)}), bf16[64,8,384]{2,0,1:T(8,128)(2,1)S(1)}, u32[]{:S(2)}, u32[]{:S(2)}) %all-to-all-start.1) | async-done | bytes 393248 | tf_op jit(solution)/shard_map/all_to_all | solution.py:135
  77.5 0.6 fusion.115
  78.6 0.7 fusion.90
  79.4 7.7 %all-gather.2.cloned.1.call-done = bf16[32,1,2,128,128]{4,3,2,1,0:T(8,128)(2,1)} async-done(((bf16[1,1,2,128,128]{4,3,2,1,0:T(8,128)(2,1)}), bf16[32,1,2,128,128]{4,3,2,1,0:T(8,128)(2,1)}) %all-gather.2.cloned.1.call-update) | async-done | bytes 2097168 | tf_op jit(solution)/shard_map/all_gather | solution.py:153
  87.1 2.1 multiply_reduce_fusion
  89.2 153.4 %all-reduce.3.cloned.1.call-done = bf16[32,32768]{1,0:T(8,128)(2,1)} async-done(((bf16[32,32768]{1,0:T(8,128)(2,1)}), bf16[32,32768]{1,0:T(8,128)(2,1)}) %all-reduce.3.cloned.1.call-update) | async-done | bytes 2097168
  242.5 1.7 fusion.93
  244.7 0.7 convolution_multiply_fusion.8
  245.4 0.7 fusion.87
  246.8 0.7 convolution_multiply_fusion.7
  247.5 0.7 fusion.84
  248.8 0.7 convolution_multiply_fusion.6
  249.6 0.7 fusion.81
  250.9 0.7 convolution_multiply_fusion.5
  251.6 0.7 fusion.78
  252.9 0.7 convolution_multiply_fusion.4
  253.6 0.7 fusion.75
  254.9 0.9 convolution_multiply_fusion.3
  255.9 0.7 fusion.72
  257.3 0.7 convolution_multiply_fusion.2
  258.0 0.7 fusion.69
  259.4 0.7 convolution_multiply_fusion.1
  260.1 0.7 fusion.65
  261.8 0.7 reduce.33
  262.6 14.3 %all_to_all.45 = bf16[8,2,4096]{2,1,0:T(2,128)(2,1)S(1)} all-to-all(bf16[8,2,4096]{2,1,0:T(2,128)(2,1)S(1)} %reshape.736), channel_id=1, replica_groups=mesh['grp'=32,'head'=8] {'head'}, dimensions={0} | all-to-all | bytes 262144 | tf_op jit(solution)/shard_map/all_to_all | solution.py:180
  277.1 2.7 fusion.24
  (114 shorter events, 9.7 us)
Async XLA Ops:
  6.5 23.1 %copy-start = (bf16[64,128,1,128]{3,1,2,0:T(8,128)(2,1)S(1)}, bf16[64,128,1,128]{3,1,2,0:T(8,128)(2,1)}, u32[]{:S(2)}) copy-start(bf16[64,128,1,128]{3,1,2,0:T(8,128)(2,1)} %param.25) | copy-start | bytes 6291460
  6.5 80.5 %all-gather.2.cloned.1.call-start = ((), (), s32[]{:S(2)}) async-start(), calls=%async_computation.3 | async-start | bytes 2162688 | tf_op jit(solution)/shard_map/all_gather | solution.py:153
  9.3 8.8 %copy-start.10 = (f32[8]{0:T(128)S(1)}, f32[8]{0:T(128)}, u32[]{:S(2)}) copy-start(f32[8]{0:T(128)} %param.21) | copy-start | bytes 100
  9.3 8.8 %copy-start.3 = (bf16[64,1024]{1,0:T(8,128)(2,1)S(1)}, bf16[64,1024]{1,0:T(8,128)(2,1)}, u32[]{:S(2)}) copy-start(bf16[64,1024]{1,0:T(8,128)(2,1)} %param.15) | copy-start | bytes 393220
  9.3 8.8 %copy-start.7 = (f32[1024]{0:T(1024)S(1)}, f32[1024]{0:T(1024)}, u32[]{:S(2)}) copy-start(f32[1024]{0:T(1024)} %param.16) | copy-start | bytes 12292
  9.3 8.8 %copy-start.9 = (bf16[1024,16]{0,1:T(8,128)(2,1)S(1)}, bf16[1024,16]{0,1:T(8,128)(2,1)}, u32[]{:S(2)}) copy-start(bf16[1024,16]{0,1:T(8,128)(2,1)} %param.18) | copy-start | bytes 98308
  9.4 13.9 %copy-start.8 = (s32[32]{0:T(128)S(1)}, s32[32]{0:T(128)}, u32[]{:S(2)}) copy-start(s32[32]{0:T(128)} %param.27) | copy-start | bytes 388
  9.4 14.0 %copy-start.5 = (s32[32,64]{1,0:T(8,128)S(1)}, s32[32,64]{1,0:T(8,128)}, u32[]{:S(2)}) copy-start(s32[32,64]{1,0:T(8,128)} %param.26) | copy-start | bytes 24580
  13.6 46.5 %collective-permute-start = (bf16[3,3072]{1,0:T(4,128)(2,1)S(1)}, bf16[3,3072]{1,0:T(4,128)(2,1)S(1)}, u32[]{:S(2)}, u32[]{:S(2)}) collective-permute-start(bf16[3,3072]{1,0:T(4,128)(2,1)S(1)} %slice.93), channel_id=1, source_target_pairs={{0,1},{1,2},{2,3},{3,4},{4,5},{5,6},{6,7},{8,9},{9,10},{10,11},{11... | collective-permute-start | bytes 55304 | tf_op jit(solution)/shard_map/ppermute | solution.py:24
  19.1 40.9 %all-to-all-start = ((bf16[64,8,2]{0,2,1:T(2,128)(2,1)}), bf16[64,8,2]{0,2,1:T(2,128)(2,1)S(1)}, u32[]{:S(2)}, u32[]{:S(2)}) async-start(bf16[64,8,2]{0,2,1:T(2,128)(2,1)} %copy.113), calls=%async_computation | async-start | bytes 8192 | tf_op jit(solution)/shard_map/all_to_all | solution.py:136
  23.2 219.3 %all-reduce.3.cloned.1.call-start = ((), (), s32[]{:S(2)}) async-start(), calls=%async_computation.4 | async-start | bytes 4194304
  24.1 5.5 %copy-start.2 = (bf16[64,128,1,128]{3,1,2,0:T(8,128)(2,1)S(1)}, bf16[64,128,1,128]{3,1,2,0:T(8,128)(2,1)}, u32[]{:S(2)}) copy-start(bf16[64,128,1,128]{3,1,2,0:T(8,128)(2,1)} %param.24) | copy-start | bytes 6291460
  55.1 0.7 copy-start.4
  55.1 2.3 copy-start.6
  55.1 2.3 copy-start.11
  55.1 4.3 %copy-start.12 = (u32[256]{0:T(256)S(1)}, u32[256]{0:T(256)}, u32[]{:S(2)}) copy-start(u32[256]{0:T(256)} %constant.84) | copy-start | bytes 3076
  64.8 12.6 %all-to-all-start.1 = ((bf16[64,8,384]{2,0,1:T(8,128)(2,1)}), bf16[64,8,384]{2,0,1:T(8,128)(2,1)S(1)}, u32[]{:S(2)}, u32[]{:S(2)}) async-start(bf16[64,8,384]{2,0,1:T(8,128)(2,1)} %copy.121), calls=%async_computation.1 | async-start | bytes 786432 | tf_op jit(solution)/shard_map/all_to_all | solution.py:135
  262.4 17.4 %copy-start.1 = (bf16[64,128,1,128]{3,1,2,0:T(8,128)(2,1)S(1)}, bf16[64,128,1,128]{3,1,2,0:T(8,128)(2,1)}, u32[]{:S(2)}) copy-start(bf16[64,128,1,128]{3,1,2,0:T(8,128)(2,1)} %param.25) | copy-start | bytes 6291460
Sparse Core Ops, SparseCore 0:
  9.9 77.0 all-gather.1
  90.6 151.9 all-reduce.2
where the time goes:
time: 288 us; the launch traced here: 287 us
  waiting for transfers between devices  169 us (59%)
  matrix products  43.5 us (15%)
  local copies, waits for them, and re-layouts  19.7 us (7%)
  between operations  14.8 us (5%)
  blocking collectives  14.3 us (5%)
  starting transfers between devices  13.4 us (5%)
  other arithmetic  12.4 us (4%)
    unnamed x3, waiting for transfers between devices  153 us
    all_to_all x1, blocking collectives, shards(): lax.all_to_all(read_out.reshape(group_rows, 1, heads_here * HDIM), 'head'...  14.3 us
    reshape x1, local copies, waits for them, and re-layouts, page_sums(): jnp.stack([page_grams, page_cross], axis=2).reshape(keys_live.shape[0], -1)  9.39 us
    dot_general x1, matrix products, shards(): jnp.dot(owner_map, per_page, precision=PRECISE, preferred_element_type=jn...  8.21 us
    all_gather x1, waiting for transfers between devices, shards(): lax.all_gather(prompt_state.astype(jnp.bfloat16), 'grp', axis=0, tiled=True)  7.69 us
    all_to_all x1, waiting for transfers between devices, shards(): lax.all_to_all(stacked, 'head', split_axis=1, concat_axis=0, tiled=True)  7.53 us
  transfers between devices with their start and end apart: 5, of which 3 were waited for; matrix products, arithmetic and copies ran while one was open for 18% of the time, Pallas kernels for 0%

commit v1 on v0

v1 whole, which is shorter than its diff:
```python
import jax
import jax.numpy as jnp
from jax import lax
from jax.experimental import pallas as pl
from jax.experimental.pallas import tpu as pltpu
from jax.sharding import PartitionSpec as P

D = 1024
HEADS = 8
HDIM = 128
CONV = 4
NEW = 512
CG_STEPS = 8
PAGE = 128
POOL_DEV = 64
NY = 4
NZ = 8
TOK = NEW // HEADS
PART = 3 * HDIM
WIDE = PART + HDIM
TAIL = 16
ROWS_A = 48
ROWS_B = HDIM - ROWS_A
EPS_NORM = 1e-06
MESH = pl.DeviceIdType.MESH
F32 = jnp.float32
BF16 = jnp.bfloat16


def dot(a, b):
    return jnp.dot(a, b, preferred_element_type=F32)


def unit_rows(block):
    return block * lax.rsqrt(jnp.sum(block * block, axis=-1, keepdims=True) + EPS_NORM)


def rms_rows(block, gain):
    wide = block.astype(F32)
    mean = jnp.mean(wide * wide, axis=-1, keepdims=True)
    return (wide * lax.rsqrt(mean + EPS_NORM) * gain).astype(BF16)


def message_ids():
    ids = {}
    for dy in range(NY):
        ids["az", 1 if dy < NY // 2 else -1, 4, dy] = len(ids)
        for far in (3, 2, 1):
            for way in (1, -1):
                ids["az", way, far, dy] = len(ids)
    for dz in range(NZ):
        ids["by", 1 if dz < NZ // 2 else -1, 2, dz] = len(ids)
        for way in (1, -1):
            ids["by", way, 1, dz] = len(ids)
    for way, far in ((1, 2), (1, 1), (-1, 1)):
        ids["ay", way, far, 0] = len(ids)
    for way, far in ((1, 4), (1, 3), (1, 2), (1, 1), (-1, 3), (-1, 2), (-1, 1)):
        ids["bz", way, far, 0] = len(ids)
    return ids


IDS = message_ids()


def front_kernel(
    low_ref,
    high_ref,
    length_ref,
    prompt_of_ref,
    decay_ref,
    tokens_ref,
    gain_ref,
    gates_ref,
    conv_ref,
    stored_ref,
    prompt_ref,
    w_hbm,
    keys_hbm,
    values_hbm,
    seq_ref,
    state_ref,
    keys,
    values,
    weights,
    own_prompt,
    term_a,
    term_b,
    sum_a,
    sum_b,
    got_az,
    got_by,
    got_ay,
    got_bz,
    tail,
    normed,
    extended,
    stage,
    page_sem,
    w_sem,
    send_sem,
    recv_sem,
    head_send,
    head_recv,
):
    grp = lax.axis_index("grp")
    head = lax.axis_index("head")
    y, z = grp // NZ, grp % NZ

    def at_z(dz):
        return {"grp": y * NZ + (z + dz + NZ) % NZ}

    def at_y(dy):
        return {"grp": (y + dy + NY) % NY * NZ + z}

    def at_head(dh):
        return {"head": (head + dh) % HEADS}

    loads = []
    pieces = 4
    span = POOL_DEV // pieces
    for i in range(pieces):
        part = pl.ds(i * span, span)
        loads.append(
            pltpu.make_async_copy(keys_hbm.at[part], keys.at[part], page_sem.at[2 * i])
        )
        loads.append(
            pltpu.make_async_copy(values_hbm.at[part], values.at[part], page_sem.at[2 * i + 1])
        )
    w_loads = []
    for dh in range(HEADS):
        off = pl.multiple_of((head + dh) % HEADS * PART, HDIM)
        w_loads.append(
            pltpu.make_async_copy(w_hbm.at[:, pl.ds(off, PART)], weights.at[dh], w_sem.at[dh])
        )
    for copy in loads:
        copy.start()
    for copy in w_loads:
        copy.start()

    barrier = pltpu.get_barrier_semaphore()
    peers = [at_z(1), at_z(-1), at_y(1), at_y(-1)] + [at_head(dh) for dh in range(1, HEADS)]
    for peer in peers:
        pl.semaphore_signal(barrier, inc=1, device_id=peer, device_id_type=MESH)

    own_prompt[:, :HDIM] = prompt_ref[0, 0, 0].T
    own_prompt[:, HDIM:] = prompt_ref[0, 0, 1].T
    normed[TAIL:] = rms_rows(tokens_ref[...], gain_ref[...])

    pl.semaphore_wait(barrier, len(peers))

    sent = []

    def remote(src, dst, send, recv, peer):
        copy = pltpu.make_async_remote_copy(
            src_ref=src,
            dst_ref=dst,
            send_sem=send,
            recv_sem=recv,
            device_id=peer,
            device_id_type=MESH,
        )
        copy.start()
        sent.append(copy)
        return copy

    tail_copy = remote(
        tokens_ref.at[pl.ds(TOK - TAIL, TAIL)], tail, head_send.at[0], head_recv.at[0], at_head(1)
    )

    flying = {}
    way_slot = {1: 0, -1: 1}

    def landing(kind, way, far, piece):
        w = way_slot[way]
        return {"az": got_az, "by": got_by, "ay": got_ay, "bz": got_bz}[kind].at[w, far - 1, piece]

    def send(kind, way, far, piece, src):
        i = IDS[kind, way, far, piece]
        peer = at_z(way) if kind in ("az", "bz") else at_y(way)
        flying[kind, way, far, piece] = remote(
            src, landing(kind, way, far, piece), send_sem.at[i], recv_sem.at[i], peer
        )

    def arrived(kind, way, far, piece):
        flying[kind, way, far, piece].wait_recv()
        return landing(kind, way, far, piece)[...].astype(F32)

    for copy in loads:
        copy.wait()

    token_row = lax.broadcasted_iota(jnp.int32, (PAGE, HDIM), 0)

    def page_pair(code, length):
        count = length - (code >> 6) * PAGE
        live = (token_row < count).astype(F32).astype(BF16)
        page = code & (POOL_DEV - 1)
        own = keys[page]
        return own * live, jnp.concatenate([own, values[page]], axis=1)

    def term(dy, dz):
        request = (y + dy) % NY * NZ + (z + dz) % NZ
        length = length_ref[request]
        k0, kv0 = page_pair(low_ref[request], length)
        k1, kv1 = page_pair(high_ref[request], length)
        total = lax.dot_general(
            jnp.concatenate([k0, k1], axis=0),
            jnp.concatenate([kv0, kv1], axis=0),
            (((0,), (0,)), ((), ())),
            preferred_element_type=F32,
        )
        total = total + own_prompt[...] * (prompt_of_ref[request] == grp).astype(F32)
        total = total.astype(BF16)
        term_a[dy, dz] = total[:ROWS_A]
        term_b[dy, dz] = total[ROWS_A:]

    def send_az(far, way, dy):
        dz = far * way % NZ
        if ("az", way, far + 1, dy) in IDS:
            got = arrived("az", way, far + 1, dy)
            term_a[dy, dz] = (term_a[dy, dz].astype(F32) + got).astype(BF16)
        send("az", way, far, dy, term_a.at[dy, dz])

    def send_by(far, way, dz):
        dy = far * way % NY
        if ("by", way, far + 1, dz) in IDS:
            got = arrived("by", way, far + 1, dz)
            term_b[dy, dz] = (term_b[dy, dz].astype(F32) + got).astype(BF16)
        send("by", way, far, dz, term_b.at[dy, dz])

    def first_way(kind, far, piece):
        return 1 if (kind, 1, far, piece) in IDS else -1

    def token_start():
        tail_copy.wait_recv()
        normed[:TAIL] = rms_rows(tail[...], gain_ref[...])
        logits = lax.dot_general(
            normed[TAIL:],
            gates_ref[...],
            (((1,), (1,)), ((), ())),
            preferred_element_type=F32,
        )
        lane = lax.broadcasted_iota(jnp.int32, (TOK, 2 * HEADS), 1)
        rate = jnp.zeros((TOK, 2 * HEADS), F32)
        for h in range(HEADS):
            rate = jnp.where(lane // 2 == h, decay_ref[h], rate)
        plus = jnp.maximum(logits, 0.0) + jnp.log1p(jnp.exp(-jnp.abs(logits)))
        return jnp.where(lane % 2 == 0, jax.nn.sigmoid(logits), -rate * plus).astype(BF16)

    def head_block(dh, gates):
        which = (head + dh) % HEADS
        off = pl.multiple_of(which * PART, HDIM)
        w_loads[dh].wait()
        slot = dh % 2
        extended[slot] = dot(normed[...], weights[dh]).astype(BF16).astype(F32)

        @pl.when(head == 0)
        def _():
            extended[slot, TAIL - CONV + 1 : TAIL] = stored_ref[0, :, pl.ds(off, PART)].astype(F32)

        taps = conv_ref[:, pl.ds(off, PART)]
        mixed = taps[CONV - 1 : CONV] * extended[slot, TAIL : TAIL + TOK]
        for lag in range(1, CONV):
            rows = extended[slot, TAIL - lag : TAIL - lag + TOK]
            mixed = mixed + taps[CONV - 1 - lag : CONV - lag] * rows
        query = unit_rows(jax.nn.silu(mixed[:, :HDIM]))
        key_vec = unit_rows(jax.nn.silu(mixed[:, HDIM : 2 * HDIM]))
        row = lax.broadcasted_iota(jnp.int32, (2 * HEADS, HDIM), 0)
        col = lax.broadcasted_iota(jnp.int32, (2 * HEADS, HDIM), 1)
        pick = (row == 2 * which + (col >= HDIM // 2).astype(jnp.int32)).astype(F32).astype(BF16)
        block = jnp.concatenate(
            [query, key_vec, mixed[:, 2 * HDIM :], dot(gates, pick)], axis=1
        ).astype(BF16)
        if dh == 0:
            seq_ref[head] = block
            return None
        stage[dh] = block
        return remote(
            stage.at[dh], seq_ref.at[head], head_send.at[dh], head_recv.at[dh], at_head(dh)
        )

    for dy in (2, 0, 1, 3):
        term(dy, 4)
        send_az(4, first_way("az", 4, dy), dy)
        if dy == 2:
            send_by(2, first_way("by", 2, 4), 4)
    for dz in (3, 5, 2, 6, 1, 7, 0):
        term(2, dz)
        send_by(2, first_way("by", 2, dz), dz)
    for dz, way in ((3, 1), (5, -1)):
        for dy in (0, 1, 3):
            term(dy, dz)
    for dy in range(NY):
        send_az(3, 1, dy)
        send_az(3, -1, dy)
    for dz in (3, 5, 4):
        send_by(1, 1, dz)
        send_by(1, -1, dz)
    gates = token_start()
    head_copies = {}
    for dz in (2, 6):
        for dy in (0, 1, 3):
            term(dy, dz)
        send_by(1, 1, dz)
        send_by(1, -1, dz)
    for dh in (1, 2):
        head_copies[dh] = head_block(dh, gates)
    for dy in range(NY):
        send_az(2, 1, dy)
        send_az(2, -1, dy)
    for dz in (1, 7, 0):
        for dy in (0, 1, 3):
            term(dy, dz)
        send_by(1, 1, dz)
        send_by(1, -1, dz)
    for dh in (3, 4):
        head_copies[dh] = head_block(dh, gates)
    for dy in range(NY):
        send_az(1, 1, dy)
        send_az(1, -1, dy)
    for dh in (5, 6):
        head_copies[dh] = head_block(dh, gates)

    def send_bz(far, way):
        dz = far * way % NZ
        total = term_b[0, dz].astype(F32) + arrived("by", 1, 1, dz) + arrived("by", -1, 1, dz)
        if ("bz", way, far + 1, 0) in IDS:
            total = total + arrived("bz", way, far + 1, 0)
        sum_b[dz] = total.astype(BF16)
        send("bz", way, far, 0, sum_b.at[dz])

    def send_ay(far, way):
        dy = far * way % NY
        total = term_a[dy, 0].astype(F32) + arrived("az", 1, 1, dy) + arrived("az", -1, 1, dy)
        if ("ay", way, far + 1, 0) in IDS:
            total = total + arrived("ay", way, far + 1, 0)
        sum_a[dy] = total.astype(BF16)
        send("ay", way, far, 0, sum_a.at[dy])

    send_bz(4, 1)
    send_bz(3, -1)
    head_copies[7] = head_block(7, gates)
    send_bz(3, 1)
    send_bz(2, -1)
    head_block(0, gates)
    send_ay(2, 1)
    send_ay(1, -1)
    send_bz(2, 1)
    send_bz(1, -1)
    send_ay(1, 1)
    send_bz(1, 1)
    rows_a = term_a[0, 0].astype(F32) + arrived("az", 1, 1, 0) + arrived("az", -1, 1, 0)
    rows_a = rows_a + arrived("ay", 1, 1, 0) + arrived("ay", -1, 1, 0)
    state_ref[:ROWS_A] = rows_a
    rows_b = term_b[0, 0].astype(F32) + arrived("by", 1, 1, 0) + arrived("by", -1, 1, 0)
    rows_b = rows_b + arrived("bz", 1, 1, 0) + arrived("bz", -1, 1, 0)
    state_ref[ROWS_A:] = rows_b

    for dh in range(1, HEADS):
        source = (head + HEADS - dh) % HEADS
        pltpu.make_async_remote_copy(
            src_ref=stage.at[dh],
            dst_ref=seq_ref.at[source],
            send_sem=head_send.at[dh],
            recv_sem=head_recv.at[dh],
            device_id=at_head(dh),
            device_id_type=MESH,
        ).wait_recv()
    for copy in sent:
        copy.wait_send()


def front(low, high, lengths, prompt_of, decay, tokens, gain, gates, conv, stored, prompt, w, keys, values):
    smem = pl.BlockSpec(memory_space=pltpu.SMEM)
    vmem = pl.BlockSpec(memory_space=pltpu.VMEM)
    hbm = pl.BlockSpec(memory_space=pl.ANY)
    dma = pltpu.SemaphoreType.DMA
    return pl.pallas_call(
        front_kernel,
        name="front",
        out_shape=(
            jax.ShapeDtypeStruct((HEADS, TOK, WIDE), BF16),
            jax.ShapeDtypeStruct((HDIM, 2 * HDIM), F32),
        ),
        in_specs=[smem] * 5 + [vmem] * 6 + [hbm] * 3,
        out_specs=(vmem, vmem),
        scratch_shapes=[
            pltpu.VMEM((POOL_DEV, PAGE, HDIM), BF16),
            pltpu.VMEM((POOL_DEV, PAGE, HDIM), BF16),
            pltpu.VMEM((HEADS, D, PART), BF16),
            pltpu.VMEM((HDIM, 2 * HDIM), F32),
            pltpu.VMEM((NY, NZ, ROWS_A, 2 * HDIM), BF16),
            pltpu.VMEM((NY, NZ, ROWS_B, 2 * HDIM), BF16),
            pltpu.VMEM((NY, ROWS_A, 2 * HDIM), BF16),
            pltpu.VMEM((NZ, ROWS_B, 2 * HDIM), BF16),
            pltpu.VMEM((2, 4, NY, ROWS_A, 2 * HDIM), BF16),
            pltpu.VMEM((2, 2, NZ, ROWS_B, 2 * HDIM), BF16),
            pltpu.VMEM((2, 2, 1, ROWS_A, 2 * HDIM), BF16),
            pltpu.VMEM((2, 4, 1, ROWS_B, 2 * HDIM), BF16),
            pltpu.VMEM((TAIL, D), BF16),
            pltpu.VMEM((TAIL + TOK, D), BF16),
            pltpu.VMEM((2, TAIL + TOK, PART), F32),
            pltpu.VMEM((HEADS, TOK, WIDE), BF16),
            dma((8,)),
            dma((HEADS,)),
            dma((len(IDS),)),
            dma((len(IDS),)),
            dma((HEADS,)),
            dma((HEADS,)),
        ],
        compiler_params=pltpu.CompilerParams(
            collective_id=0, has_side_effects=True, vmem_limit_bytes=56 * 2**20
        ),
    )(low, high, lengths, prompt_of, decay, tokens, gain, gates, conv, stored, prompt, w, keys, values)


def solve_kernel(ridge_ref, seq_ref, state_ref, out_ref, keys_t, weights, start, solved, residue, direction):
    ridge = ridge_ref[0]
    gates = seq_ref[:, PART:]
    half = HDIM // 2
    lower = lax.broadcasted_iota(jnp.int32, (NEW, NEW), 0) >= lax.broadcasted_iota(
        jnp.int32, (NEW, NEW), 1
    )
    cumul = dot(lower.astype(F32).astype(BF16), gates)
    cumul_row = cumul.T[half : half + 1]
    gate_row = gates.astype(F32).T[0:1]
    cumul_col = cumul[:, half : half + 1]
    carry = jnp.exp(cumul_col)
    keys_t[...] = seq_ref[:, HDIM : 2 * HDIM].astype(F32).T.astype(BF16)
    start[...] = state_ref[...].astype(BF16)
    blocks = NEW // HDIM
    diagonal = lax.broadcasted_iota(jnp.int32, (HDIM, HDIM), 0) >= lax.broadcasted_iota(
        jnp.int32, (HDIM, HDIM), 1
    )
    for b in range(blocks):
        rows = slice(b * HDIM, (b + 1) * HDIM)
        for a in range(b + 1):
            cols = slice(a * HDIM, (a + 1) * HDIM)
            spread = cumul_col[rows] - cumul_row[:, cols]
            if a == b:
                spread = jnp.where(diagonal, spread, -jnp.inf)
            weights[rows, cols] = jnp.exp(spread) * gate_row[:, cols]
    query = seq_ref[:, :HDIM].astype(F32)
    solved[...] = jnp.zeros_like(solved)
    residue[...] = query
    direction[...] = query
    norms = tuple(
        jnp.sum(query[b * HDIM : (b + 1) * HDIM] ** 2, axis=-1, keepdims=True) for b in range(blocks)
    )

    def read(b, vectors, table, against):
        rows, seen = slice(b * HDIM, (b + 1) * HDIM), (b + 1) * HDIM
        scores = dot(vectors.astype(BF16), keys_t[:, :seen]) * weights[rows, :seen]
        opening = dot((carry[rows] * vectors).astype(BF16), table)
        return opening + dot(scores.astype(BF16), against[:seen])

    key_rows = seq_ref[:, HDIM : 2 * HDIM]

    def step(_, norms):
        following = []
        for b in range(blocks):
            rows = slice(b * HDIM, (b + 1) * HDIM)
            ahead = direction[rows]
            image = read(b, ahead, start[:, :HDIM], key_rows) + ridge * ahead
            alpha = norms[b] / jnp.sum(ahead * image, axis=-1, keepdims=True)
            solved[rows] = solved[rows] + alpha * ahead
            left = residue[rows] - alpha * image
            norm = jnp.sum(left * left, axis=-1, keepdims=True)
            residue[rows] = left
            direction[rows] = left + norm / norms[b] * ahead
            following.append(norm)
        return tuple(following)

    lax.fori_loop(0, CG_STEPS, step, norms)
    for b in range(blocks):
        rows = slice(b * HDIM, (b + 1) * HDIM)
        result = read(b, solved[rows], start[:, HDIM:], seq_ref[:, 2 * HDIM : PART])
        out_ref[rows] = result.astype(BF16)


def solve(ridge, seq, state):
    smem = pl.BlockSpec(memory_space=pltpu.SMEM)
    vmem = pl.BlockSpec(memory_space=pltpu.VMEM)
    return pl.pallas_call(
        solve_kernel,
        name="solve",
        out_shape=jax.ShapeDtypeStruct((NEW, HDIM), BF16),
        in_specs=[smem, vmem, vmem],
        out_specs=vmem,
        scratch_shapes=[
            pltpu.VMEM((HDIM, NEW), BF16),
            pltpu.VMEM((NEW, NEW), F32),
            pltpu.VMEM((HDIM, 2 * HDIM), BF16),
            pltpu.VMEM((NEW, HDIM), F32),
            pltpu.VMEM((NEW, HDIM), F32),
            pltpu.VMEM((NEW, HDIM), F32),
        ],
        compiler_params=pltpu.CompilerParams(vmem_limit_bytes=32 * 2**20),
    )(ridge, seq, state)


def back_kernel(read_ref, tokens_ref, w_hbm, out_ref, weights, got, w_sem, send_sem, recv_sem):
    head = lax.axis_index("head")
    load = pltpu.make_async_copy(w_hbm, weights, w_sem)
    load.start()
    barrier = pltpu.get_barrier_semaphore()
    for dh in range(1, HEADS):
        pl.semaphore_signal(
            barrier, inc=1, device_id={"head": (head + dh) % HEADS}, device_id_type=MESH
        )
    pl.semaphore_wait(barrier, HEADS - 1)
    copies = []
    for dh in range(1, HEADS):
        peer = (head + dh) % HEADS
        copy = pltpu.make_async_remote_copy(
            src_ref=read_ref.at[peer],
            dst_ref=got.at[head],
            send_sem=send_sem.at[dh],
            recv_sem=recv_sem.at[dh],
            device_id={"head": peer},
            device_id_type=MESH,
        )
        copy.start()
        copies.append(copy)
    got[head] = read_ref[head]
    load.wait()
    for dh in range(1, HEADS):
        source = (head + HEADS - dh) % HEADS
        pltpu.make_async_remote_copy(
            src_ref=read_ref.at[source],
            dst_ref=got.at[source],
            send_sem=send_sem.at[dh],
            recv_sem=recv_sem.at[dh],
            device_id={"head": source},
            device_id_type=MESH,
        ).wait_recv()
    rows = jnp.concatenate([got[h] for h in range(HEADS)], axis=1)
    out_ref[...] = (tokens_ref[...].astype(F32) + dot(rows, weights[...])).astype(BF16)
    for copy in copies:
        copy.wait_send()


def back(read_out, tokens, w_out):
    vmem = pl.BlockSpec(memory_space=pltpu.VMEM)
    return pl.pallas_call(
        back_kernel,
        name="back",
        out_shape=jax.ShapeDtypeStruct((TOK, D), BF16),
        in_specs=[vmem, vmem, pl.BlockSpec(memory_space=pl.ANY)],
        out_specs=vmem,
        scratch_shapes=[
            pltpu.VMEM((HEADS * HDIM, D), BF16),
            pltpu.VMEM((HEADS, TOK, HDIM), BF16),
            pltpu.SemaphoreType.DMA,
            pltpu.SemaphoreType.DMA((HEADS,)),
            pltpu.SemaphoreType.DMA((HEADS,)),
        ],
        compiler_params=pltpu.CompilerParams(
            collective_id=1, has_side_effects=True, vmem_limit_bytes=32 * 2**20
        ),
    )(read_out, tokens, w_out)


def shards(
    tokens,
    norm_gain,
    w_qkv,
    w_gates,
    conv_weight,
    conv_state,
    decay_rate,
    ridge,
    w_out,
    cache_keys,
    cache_values,
    page_table,
    cache_lengths,
    group_prompt,
    prompt_state,
):
    local = page_table - lax.axis_index("grp") * POOL_DEV
    here = (local >= 0) & (local < POOL_DEV)
    code = jnp.arange(page_table.shape[1])[None, :] * POOL_DEV + local
    low = jnp.min(jnp.where(here, code, 1 << 20), axis=1)
    high = jnp.max(jnp.where(here, code, -1), axis=1)
    seq, state = front(
        low,
        high,
        cache_lengths,
        group_prompt,
        decay_rate,
        tokens,
        norm_gain.reshape(1, D),
        w_gates.T,
        conv_weight,
        conv_state,
        prompt_state,
        w_qkv,
        cache_keys.reshape(POOL_DEV, PAGE, HDIM),
        cache_values.reshape(POOL_DEV, PAGE, HDIM),
    )
    read_out = solve(ridge, seq.reshape(NEW, WIDE), state)
    return back(read_out.reshape(HEADS, TOK, HDIM), tokens, w_out)


def solution(mesh):
    placed = (
        P(("grp", "head"), None),
        P(),
        P(),
        P(),
        P(),
        P("grp", None, None),
        P(),
        P("head"),
        P(),
        P("grp", None, "head", None),
        P("grp", None, "head", None),
        P(),
        P(),
        P(),
        P("grp", "head", None, None, None),
    )
    return jax.shard_map(
        shards, mesh=mesh, in_specs=placed, out_specs=P(("grp", "head"), None), check_vma=False
    )
```

time: 288 us -> 59.5 us (0.21)
  waiting for transfers between devices: 169 us -> 0 us
  Pallas kernels: 0 us -> 54.5 us
  matrix products: 43.5 us -> 0 us
  local copies, waits for them, and re-layouts: 19.7 us -> 2.6 us
  blocking collectives: 14.3 us -> 0 us
  between operations: 14.8 us -> 0.71 us
  starting transfers between devices: 13.4 us -> 0 us
  other arithmetic: 12.4 us -> 1.41 us
    unnamed x3 -> x0, waiting for transfers between devices: 153 us -> none
    pallas_call x0 -> x3, Pallas kernels: none -> 54.5 us  [the longest x1 33.6 us: front(): pl.pallas_call(front_kernel, name='front', out_shape=(jax.ShapeDtypeStruc...]
    dot_general x37 -> x0, matrix products: 43.5 us -> none  [the longest x1 8.21 us: shards(): jnp.dot(owner_map, per_page, precision=PRECISE, preferred_element_type=jn...]
    all_to_all x1 -> x0, blocking collectives: 14.3 us -> none  [shards(): lax.all_to_all(read_out.reshape(group_rows, 1, heads_here * HDIM), 'head'...]
    reshape x3 -> x0, local copies, waits for them, and re-layouts: 10.1 us -> none  [the longest x1 9.39 us: page_sums(): jnp.stack([page_grams, page_cross], axis=2).reshape(keys_live.shape[0], -1)]
    all_to_all x2 -> x0, starting transfers between devices: 8.93 us -> none  [the longest x1 4.81 us: shards(): lax.all_to_all(stacked, 'head', split_axis=1, concat_axis=0, tiled=True)]
    all_gather x1 -> x0, waiting for transfers between devices: 7.69 us -> none  [shards(): lax.all_gather(prompt_state.astype(jnp.bfloat16), 'grp', axis=0, tiled=True)]
    all_to_all x2 -> x0, waiting for transfers between devices: 7.53 us -> none  [the longest x1 7.53 us: shards(): lax.all_to_all(stacked, 'head', split_axis=1, concat_axis=0, tiled=True)]
  transfers between devices with their start and end apart: 5 -> 0, of which waited for: 3 -> 0; matrix products, arithmetic and copies ran while one was open for 18% -> 0% of each run, Pallas kernels for 0% -> 0%
where the time goes in v1:
time: 59.5 us; the launch traced here: 59.2 us
  Pallas kernels  54.5 us (92%)
  local copies, waits for them, and re-layouts  2.6 us (4%)
  other arithmetic  1.41 us (2%)
  between operations  0.71 us (1%)
    pallas_call x1, Pallas kernels, front(): pl.pallas_call(front_kernel, name='front', out_shape=(jax.ShapeDtypeStruc...  33.6 us
    pallas_call x1, Pallas kernels, back(): pl.pallas_call(back_kernel, name='back', out_shape=jax.ShapeDtypeStruct((...  13.4 us
    pallas_call x1, Pallas kernels, solve(): pl.pallas_call(solve_kernel, name='solve', out_shape=jax.ShapeDtypeStruct...  7.51 us
    unnamed x9, local copies, waits for them, and re-layouts  2.6 us
    reduce_max x1, other arithmetic, shards(): high = jnp.max(jnp.where(here, code, -1), axis=1)  1.41 us

profile of v1, /device:TPU:1, one launch (start us, length us, event | category | flops | bytes accessed | tf_op | source)
XLA Modules:
  0.0 59.2 jit_solution(2624447769824580237)
XLA Ops:
  0.7 1.4 %select_reduce_fusion = (s32[32]{0:T(128)}, s32[32]{0:T(128)}) fusion(s32[32,64]{1,0:T(8,128)} %param.26, s32[64]{0:T(128)S(1)} %iota_multiply_fusion, s32[]{:T(128)S(6)} %mul.14), kind=kLoop, calls=%fused_computation | loop fusion | flops 18368 | bytes 8708 | tf_op jit(solution)/shard_map/reduce_max | solution.py:584
  2.1 0.0 copy-start
  2.1 0.0 copy-start.1
  2.1 33.6 %front.1 = (bf16[8,64,512]{2,1,0:T(8,128)(2,1)}, f32[128,256]{1,0:T(8,128)}) custom-call(s32[32]{0:T(128)} %get-tuple-element.10.low_ref, s32[32]{0:T(128)} %get-tuple-element.9.high_ref, s32[32]{0:T(128)} %length_ref.1, s32[32]{0:T(128)} %prompt_of_ref.1, f32[8]{0:T(128)} %decay_ref.1, bf16[64,1024]{1,0:T(8,128)(2,1)} %tokens_ref.3, f32[1,1024]{1,0:T(1,128)} %bitcast.11, ...), custom_call_target="tpu_custom_call" | custom-call | tf_op jit(solution)/shard_map/front/pallas_call | solution.py:377
  35.7 0.0 copy-start.2
  35.7 1.0 %copy-done.2 = bf16[8,64,512]{2,1,0:T(8,128)(2,1)S(1)} copy-done((bf16[8,64,512]{2,1,0:T(8,128)(2,1)S(1)}, bf16[8,64,512]{2,1,0:T(8,128)(2,1)}, u32[]{:S(2)}) %copy-start.2) | copy-done | bytes 524312
  36.7 0.0 copy-start.3
  36.8 0.9 %copy-done.3 = f32[128,256]{1,0:T(8,128)S(1)} copy-done((f32[128,256]{1,0:T(8,128)S(1)}, f32[128,256]{1,0:T(8,128)}, u32[]{:S(2)}) %copy-start.3) | copy-done | bytes 131096
  37.7 7.5 %solve.1 = bf16[512,128]{1,0:T(8,128)(2,1)S(1)} custom-call(f32[1]{0:T(128)S(6)} %copy.17.ridge_ref, bf16[512,512]{1,0:T(8,128)(2,1)S(1)} %bitcast.6, f32[128,256]{1,0:T(8,128)S(1)} %copy-done.3), custom_call_target="tpu_custom_call" | custom-call | tf_op jit(solution)/shard_map/solve/pallas_call | solution.py:483
  45.2 0.0 copy-done
  45.2 0.0 copy-done.1
  45.2 13.4 %back.1 = bf16[64,1024]{1,0:T(8,128)(2,1)S(1)} custom-call(bf16[8,64,128]{2,1,0:T(8,128)(2,1)S(1)} %bitcast.7, bf16[64,1024]{1,0:T(8,128)(2,1)S(1)} %copy-done.1, bf16[1024,1024]{1,0:T(8,128)(2,1)S(1)} %copy-done), custom_call_target="tpu_custom_call" | custom-call | tf_op jit(solution)/shard_map/back/pallas_call | solution.py:544
  58.6 0.7 %copy.18 = bf16[64,1024]{1,0:T(8,128)(2,1)} copy(bf16[64,1024]{1,0:T(8,128)(2,1)S(1)} %back.1) | data formatting | bytes 262144
  (1 shorter events, 0.0 us)
Async XLA Ops:
  2.1 43.1 %copy-start = (bf16[1024,1024]{1,0:T(8,128)(2,1)S(1)}, bf16[1024,1024]{1,0:T(8,128)(2,1)}, u32[]{:S(2)}) copy-start(bf16[1024,1024]{1,0:T(8,128)(2,1)} %w_hbm.3) | copy-start | bytes 6291460
  2.1 43.1 %copy-start.1 = (bf16[64,1024]{1,0:T(8,128)(2,1)S(1)}, bf16[64,1024]{1,0:T(8,128)(2,1)}, u32[]{:S(2)}) copy-start(bf16[64,1024]{1,0:T(8,128)(2,1)} %tokens_ref.3) | copy-start | bytes 393220
  35.7 1.0 %copy-start.2 = (bf16[8,64,512]{2,1,0:T(8,128)(2,1)S(1)}, bf16[8,64,512]{2,1,0:T(8,128)(2,1)}, u32[]{:S(2)}) copy-start(bf16[8,64,512]{2,1,0:T(8,128)(2,1)} %get-tuple-element.7) | copy-start | bytes 1572868
  36.7 0.9 %copy-start.3 = (f32[128,256]{1,0:T(8,128)S(1)}, f32[128,256]{1,0:T(8,128)}, u32[]{:S(2)}) copy-start(f32[128,256]{1,0:T(8,128)} %get-tuple-element.8.state_ref) | copy-start | bytes 393220

commit v2 on v1

v2 whole, which is shorter than its diff:
```python
import jax
import jax.numpy as jnp
from jax import lax
from jax.experimental import pallas as pl
from jax.experimental.pallas import tpu as pltpu
from jax.sharding import PartitionSpec as P

D = 1024
HEADS = 8
HDIM = 128
CONV = 4
NEW = 512
CG_STEPS = 8
PAGE = 128
POOL_DEV = 64
NY = 4
NZ = 8
TOK = NEW // HEADS
PART = 3 * HDIM
WIDE = PART + HDIM
TAIL = 16
ROWS_A = 48
ROWS_B = HDIM - ROWS_A
EPS_NORM = 1e-06
MESH = pl.DeviceIdType.MESH
F32 = jnp.float32
BF16 = jnp.bfloat16


def dot(a, b):
    return jnp.dot(a, b, preferred_element_type=F32)


def unit_rows(block):
    return block * lax.rsqrt(jnp.sum(block * block, axis=-1, keepdims=True) + EPS_NORM)


def rms_rows(block, gain):
    wide = block.astype(F32)
    mean = jnp.mean(wide * wide, axis=-1, keepdims=True)
    return (wide * lax.rsqrt(mean + EPS_NORM) * gain).astype(BF16)


def task_table():
    tasks = {}

    def add(name, cost, after=(), waits=(), link=None, size=0):
        tasks[name] = (cost, tuple(after), tuple(waits), link, size)

    size_a, size_b = ROWS_A * 4 * HDIM, ROWS_B * 4 * HDIM
    for dy in range(NY):
        for dz in range(NZ):
            add(("term", dy, dz), 0.1)
    for dy in range(NY):
        for way in (1, -1):
            for far in (4, 3, 2, 1):
                if far == 4 and (way == 1) != (dy < NY // 2):
                    continue
                before = [("az", way, far + 1, dy)]
                before = [m for m in before if m in tasks]
                add(("az", way, far, dy), 0.03, [("term", dy, far * way % NZ)], before, ("z", way), size_a)
    for dz in range(NZ):
        for way in (1, -1):
            for far in (2, 1):
                if far == 2 and (way == 1) != (dz < NZ // 2):
                    continue
                before = [("by", way, far + 1, dz)]
                before = [m for m in before if m in tasks]
                add(("by", way, far, dz), 0.03, [("term", far * way % NY, dz)], before, ("y", way), size_b)
    for way, far in ((1, 2), (1, 1), (-1, 1)):
        dy = far * way % NY
        before = [("az", 1, 1, dy), ("az", -1, 1, dy)]
        before += [m for m in [("ay", way, far + 1, 0)] if m in tasks]
        add(("ay", way, far, 0), 0.03, [("term", dy, 0)], before, ("y", way), size_a)
    for way, far in ((1, 4), (1, 3), (1, 2), (1, 1), (-1, 3), (-1, 2), (-1, 1)):
        dz = far * way % NZ
        before = [("by", 1, 1, dz), ("by", -1, 1, dz)]
        before += [m for m in [("bz", way, far + 1, 0)] if m in tasks]
        add(("bz", way, far, 0), 0.03, [("term", 0, dz)], before, ("z", way), size_b)
    add(("tokens",), 0.35)
    for i in range(HEADS):
        dh = (i + 1) % HEADS
        add(("head", dh), 0.33, [("tokens",)], (), ("x", dh) if dh else None, 40000)
    add(("ready", 0), 0.5, [("head", 0)], [("head", dh) for dh in range(1, HEADS)])
    for b in range(NEW // HDIM):
        add(("ready", b + 1), 0.2, [("ready", 0)])
    last = [("az", way, 1, 0) for way in (1, -1)] + [("ay", way, 1, 0) for way in (1, -1)]
    last += [("by", way, 1, 0) for way in (1, -1)] + [("bz", way, 1, 0) for way in (1, -1)]
    add(("end",), 0.05, [("term", 0, 0)] + [("ready", b) for b in range(NEW // HDIM + 1)], last)
    return tasks


def task_order(tasks, hop=1.7, rate=46500.0, backlog=0.9):
    longest = {}
    for name in reversed(list(tasks)):
        longest[name] = tasks[name][0]
    for _ in range(12):
        for name, (cost, after, waits, _, _) in tasks.items():
            for m in after:
                longest[m] = max(longest[m], tasks[m][0] + longest[name])
            for m in waits:
                flight = hop + tasks[m][4] / rate
                longest[m] = max(longest[m], tasks[m][0] + flight + longest[name])
    now, order, landed, free = 0.0, [], {}, {}
    left = dict(tasks)
    while left:
        best, soonest = None, 1e9
        for name, (cost, after, waits, link, size) in left.items():
            if any(m in left for m in after) or any(m not in landed for m in waits):
                continue
            ready = max([landed[m] for m in waits] + [free.get(link, 0.0) - backlog])
            if ready > now:
                soonest = min(soonest, ready)
            elif best is None or longest[name] > longest[best]:
                best = name
        if best is None:
            now = soonest
            continue
        cost, _, _, link, size = left.pop(best)
        order.append(best)
        now += cost
        if link is not None:
            free[link] = max(now, free.get(link, 0.0)) + size / rate
            landed[best] = free[link] + hop
    return order


TASKS = task_table()
ORDER = task_order(TASKS)
IDS = {}
for task in TASKS:
    if task[0] in ("az", "by", "ay", "bz"):
        IDS[task] = len(IDS)


def layer_kernel(
    low_ref,
    high_ref,
    length_ref,
    prompt_of_ref,
    decay_ref,
    ridge_ref,
    tokens_ref,
    gain_ref,
    gates_ref,
    conv_ref,
    stored_ref,
    prompt_ref,
    w_hbm,
    keys_hbm,
    values_hbm,
    out_hbm,
    out_ref,
    seq_ref,
    start,
    keys,
    values,
    weights,
    own_prompt,
    term_a,
    term_b,
    sum_a,
    sum_b,
    got_az,
    got_by,
    got_ay,
    got_bz,
    tail,
    normed,
    extended,
    stage,
    page_sem,
    w_sem,
    send_sem,
    recv_sem,
    head_send,
    head_recv,
    keys_t,
    scales,
    rows_ref,
    carry,
    solved,
    residue,
    direction,
    out_w,
    read_rows,
    got,
    out_sem,
    back_send,
    back_recv,
):
    grp = lax.axis_index("grp")
    head = lax.axis_index("head")
    y, z = grp // NZ, grp % NZ

    def at_z(dz):
        return {"grp": y * NZ + (z + dz + NZ) % NZ}

    def at_y(dy):
        return {"grp": (y + dy + NY) % NY * NZ + z}

    def at_head(dh):
        return {"head": (head + dh) % HEADS}

    loads = []
    pieces = 4
    span = POOL_DEV // pieces
    for i in range(pieces):
        part = pl.ds(i * span, span)
        loads.append(
            pltpu.make_async_copy(keys_hbm.at[part], keys.at[part], page_sem.at[2 * i])
        )
        loads.append(
            pltpu.make_async_copy(values_hbm.at[part], values.at[part], page_sem.at[2 * i + 1])
        )
    w_loads = []
    for dh in range(HEADS):
        off = pl.multiple_of((head + dh) % HEADS * PART, HDIM)
        w_loads.append(
            pltpu.make_async_copy(w_hbm.at[:, pl.ds(off, PART)], weights.at[dh], w_sem.at[dh])
        )
    for copy in loads:
        copy.start()
    for copy in w_loads:
        copy.start()
    out_load = pltpu.make_async_copy(out_hbm, out_w, out_sem)
    out_load.start()

    barrier = pltpu.get_barrier_semaphore()
    peers = [at_z(1), at_z(-1), at_y(1), at_y(-1)] + [at_head(dh) for dh in range(1, HEADS)]
    for peer in peers:
        pl.semaphore_signal(barrier, inc=1, device_id=peer, device_id_type=MESH)

    own_prompt[:, :HDIM] = prompt_ref[0, 0, 0].T
    own_prompt[:, HDIM:] = prompt_ref[0, 0, 1].T
    normed[TAIL:] = rms_rows(tokens_ref[...], gain_ref[...])

    pl.semaphore_wait(barrier, len(peers))

    sent = []

    def remote(src, dst, send, recv, peer):
        copy = pltpu.make_async_remote_copy(
            src_ref=src,
            dst_ref=dst,
            send_sem=send,
            recv_sem=recv,
            device_id=peer,
            device_id_type=MESH,
        )
        copy.start()
        sent.append(copy)
        return copy

    tail_copy = remote(
        tokens_ref.at[pl.ds(TOK - TAIL, TAIL)], tail, head_send.at[0], head_recv.at[0], at_head(1)
    )

    flying = {}
    way_slot = {1: 0, -1: 1}

    def landing(kind, way, far, piece):
        w = way_slot[way]
        return {"az": got_az, "by": got_by, "ay": got_ay, "bz": got_bz}[kind].at[w, far - 1, piece]

    def send(kind, way, far, piece, src):
        i = IDS[kind, way, far, piece]
        peer = at_z(way) if kind in ("az", "bz") else at_y(way)
        flying[kind, way, far, piece] = remote(
            src, landing(kind, way, far, piece), send_sem.at[i], recv_sem.at[i], peer
        )

    def arrived(kind, way, far, piece):
        flying[kind, way, far, piece].wait_recv()
        return landing(kind, way, far, piece)[...].astype(F32)

    for copy in loads:
        copy.wait()

    token_row = lax.broadcasted_iota(jnp.int32, (PAGE, HDIM), 0)

    def page_pair(code, length):
        count = length - (code >> 6) * PAGE
        live = (token_row < count).astype(F32).astype(BF16)
        page = code & (POOL_DEV - 1)
        own = keys[page]
        return own * live, jnp.concatenate([own, values[page]], axis=1)

    def term(dy, dz):
        request = (y + dy) % NY * NZ + (z + dz) % NZ
        length = length_ref[request]
        k0, kv0 = page_pair(low_ref[request], length)
        k1, kv1 = page_pair(high_ref[request], length)
        total = lax.dot_general(
            jnp.concatenate([k0, k1], axis=0),
            jnp.concatenate([kv0, kv1], axis=0),
            (((0,), (0,)), ((), ())),
            preferred_element_type=F32,
        )
        total = total + own_prompt[...] * (prompt_of_ref[request] == grp).astype(F32)
        total = total.astype(BF16)
        term_a[dy, dz] = total[:ROWS_A]
        term_b[dy, dz] = total[ROWS_A:]

    def send_az(far, way, dy):
        dz = far * way % NZ
        if ("az", way, far + 1, dy) in IDS:
            got = arrived("az", way, far + 1, dy)
            term_a[dy, dz] = (term_a[dy, dz].astype(F32) + got).astype(BF16)
        send("az", way, far, dy, term_a.at[dy, dz])

    def send_by(far, way, dz):
        dy = far * way % NY
        if ("by", way, far + 1, dz) in IDS:
            got = arrived("by", way, far + 1, dz)
            term_b[dy, dz] = (term_b[dy, dz].astype(F32) + got).astype(BF16)
        send("by", way, far, dz, term_b.at[dy, dz])

    def first_way(kind, far, piece):
        return 1 if (kind, 1, far, piece) in IDS else -1

    def token_start():
        tail_copy.wait_recv()
        normed[:TAIL] = rms_rows(tail[...], gain_ref[...])
        logits = lax.dot_general(
            normed[TAIL:],
            gates_ref[...],
            (((1,), (1,)), ((), ())),
            preferred_element_type=F32,
        )
        lane = lax.broadcasted_iota(jnp.int32, (TOK, 2 * HEADS), 1)
        rate = jnp.zeros((TOK, 2 * HEADS), F32)
        for h in range(HEADS):
            rate = jnp.where(lane // 2 == h, decay_ref[h], rate)
        plus = jnp.maximum(logits, 0.0) + jnp.log1p(jnp.exp(-jnp.abs(logits)))
        return jnp.where(lane % 2 == 0, jax.nn.sigmoid(logits), -rate * plus).astype(BF16)

    def head_block(dh, gates):
        which = (head + dh) % HEADS
        off = pl.multiple_of(which * PART, HDIM)
        w_loads[dh].wait()
        slot = dh % 2
        extended[slot] = dot(normed[...], weights[dh]).astype(BF16).astype(F32)

        @pl.when(head == 0)
        def _():
            extended[slot, TAIL - CONV + 1 : TAIL] = stored_ref[0, :, pl.ds(off, PART)].astype(F32)

        taps = conv_ref[:, pl.ds(off, PART)]
        mixed = taps[CONV - 1 : CONV] * extended[slot, TAIL : TAIL + TOK]
        for lag in range(1, CONV):
            rows = extended[slot, TAIL - lag : TAIL - lag + TOK]
            mixed = mixed + taps[CONV - 1 - lag : CONV - lag] * rows
        query = unit_rows(jax.nn.silu(mixed[:, :HDIM]))
        key_vec = unit_rows(jax.nn.silu(mixed[:, HDIM : 2 * HDIM]))
        row = lax.broadcasted_iota(jnp.int32, (2 * HEADS, HDIM), 0)
        col = lax.broadcasted_iota(jnp.int32, (2 * HEADS, HDIM), 1)
        pick = (row == 2 * which + (col >= HDIM // 2).astype(jnp.int32)).astype(F32).astype(BF16)
        block = jnp.concatenate(
            [query, key_vec, mixed[:, 2 * HDIM :], dot(gates, pick)], axis=1
        ).astype(BF16)
        if dh == 0:
            seq_ref[head] = block
            return None
        stage[dh] = block
        return remote(
            stage.at[dh], seq_ref.at[head], head_send.at[dh], head_recv.at[dh], at_head(dh)
        )

    def send_bz(far, way):
        dz = far * way % NZ
        total = term_b[0, dz].astype(F32) + arrived("by", 1, 1, dz) + arrived("by", -1, 1, dz)
        if ("bz", way, far + 1, 0) in IDS:
            total = total + arrived("bz", way, far + 1, 0)
        sum_b[dz] = total.astype(BF16)
        send("bz", way, far, 0, sum_b.at[dz])

    def send_ay(far, way):
        dy = far * way % NY
        total = term_a[dy, 0].astype(F32) + arrived("az", 1, 1, dy) + arrived("az", -1, 1, dy)
        if ("ay", way, far + 1, 0) in IDS:
            total = total + arrived("ay", way, far + 1, 0)
        sum_a[dy] = total.astype(BF16)
        send("ay", way, far, 0, sum_a.at[dy])

    def all_heads():
        for dh in range(1, HEADS):
            source = (head + HEADS - dh) % HEADS
            pltpu.make_async_remote_copy(
                src_ref=stage.at[dh],
                dst_ref=seq_ref.at[source],
                send_sem=head_send.at[dh],
                recv_sem=head_recv.at[dh],
                device_id=at_head(dh),
                device_id_type=MESH,
            ).wait_recv()

    blocks = NEW // HDIM

    def part_of(first):
        return seq_ref[:, :, first : first + HDIM].reshape(NEW, HDIM)

    def prepare():
        all_heads()
        gates = part_of(PART)
        half = HDIM // 2
        row = lax.broadcasted_iota(jnp.int32, (HDIM, HDIM), 0)
        spread_out = dot(gates, (row == half).astype(F32).astype(BF16)).astype(BF16)
        lower = lax.broadcasted_iota(jnp.int32, (NEW, NEW), 0) >= lax.broadcasted_iota(
            jnp.int32, (NEW, NEW), 1
        )
        cumul = dot(lower.astype(F32).astype(BF16), spread_out)
        carry[...] = cumul
        rows_ref[0:1] = cumul.T[0:1]
        rows_ref[1:2] = gates.astype(F32).T[0:1]
        keys_t[...] = part_of(HDIM).astype(F32).T.astype(BF16)
        query = part_of(0).astype(F32)
        solved[...] = jnp.zeros_like(solved)
        residue[...] = query
        direction[...] = query

    def scale_rows(b):
        rows = slice(b * HDIM, (b + 1) * HDIM)
        for a in range(b + 1):
            cols = slice(a * HDIM, (a + 1) * HDIM)
            spread = carry[rows] - rows_ref[0:1, cols]
            if a == b:
                causal = lax.broadcasted_iota(
                    jnp.int32, (HDIM, HDIM), 0
                ) >= lax.broadcasted_iota(jnp.int32, (HDIM, HDIM), 1)
                spread = jnp.where(causal, spread, -jnp.inf)
            scales[rows, cols] = jnp.exp(spread) * rows_ref[1:2, cols]
        carry[rows] = jnp.exp(carry[rows])

    def close():
        rows_a = term_a[0, 0].astype(F32) + arrived("az", 1, 1, 0) + arrived("az", -1, 1, 0)
        rows_a = rows_a + arrived("ay", 1, 1, 0) + arrived("ay", -1, 1, 0)
        start[:ROWS_A] = rows_a.astype(BF16)
        rows_b = term_b[0, 0].astype(F32) + arrived("by", 1, 1, 0) + arrived("by", -1, 1, 0)
        rows_b = rows_b + arrived("bz", 1, 1, 0) + arrived("bz", -1, 1, 0)
        start[ROWS_A:] = rows_b.astype(BF16)

    gates = None
    for task in ORDER:
        kind = task[0]
        if kind == "term":
            term(task[1], task[2])
        elif kind == "az":
            send_az(task[2], task[1], task[3])
        elif kind == "by":
            send_by(task[2], task[1], task[3])
        elif kind == "ay":
            send_ay(task[2], task[1])
        elif kind == "bz":
            send_bz(task[2], task[1])
        elif kind == "tokens":
            gates = token_start()
        elif kind == "head":
            head_block(task[1], gates)
        elif kind == "ready":
            prepare() if task[1] == 0 else scale_rows(task[1] - 1)
        else:
            close()

    ridge = ridge_ref[0]

    def read(b, vectors, table, against):
        rows, seen = slice(b * HDIM, (b + 1) * HDIM), (b + 1) * HDIM
        scores = dot(vectors.astype(BF16), keys_t[:, :seen]) * scales[rows, :seen]
        opening = dot((carry[rows] * vectors).astype(BF16), table)
        return opening + dot(scores.astype(BF16), against[:seen])

    key_rows = part_of(HDIM)

    def step(_, norms):
        following = []
        for b in range(blocks):
            rows = slice(b * HDIM, (b + 1) * HDIM)
            ahead = direction[rows]
            image = read(b, ahead, start[:, :HDIM], key_rows) + ridge * ahead
            alpha = norms[b] / jnp.sum(ahead * image, axis=-1, keepdims=True)
            solved[rows] = solved[rows] + alpha * ahead
            left = residue[rows] - alpha * image
            norm = jnp.sum(left * left, axis=-1, keepdims=True)
            residue[rows] = left
            direction[rows] = left + norm / norms[b] * ahead
            following.append(norm)
        return tuple(following)

    norms = []
    for b in range(blocks):
        query = residue[b * HDIM : (b + 1) * HDIM]
        norms.append(jnp.sum(query * query, axis=-1, keepdims=True))
    lax.fori_loop(0, CG_STEPS, step, tuple(norms))
    for b in range(blocks):
        rows = slice(b * HDIM, (b + 1) * HDIM)
        result = read(b, solved[rows], start[:, HDIM:], part_of(2 * HDIM)).astype(BF16)
        read_rows[2 * b] = result[:TOK]
        read_rows[2 * b + 1] = result[TOK:]
    for dh in range(1, HEADS):
        peer = (head + dh) % HEADS
        remote(read_rows.at[peer], got.at[head], back_send.at[dh], back_recv.at[dh], at_head(dh))
    got[head] = read_rows[head]
    out_load.wait()
    total = tokens_ref[...].astype(F32)
    chip, core = head // 2, head % 2
    for dx in (0, 1, 3, 2):
        there = (chip + dx) % 4
        for c in range(2):
            source = there * 2 + c

            @pl.when(source != head)
            def _():
                pltpu.make_async_remote_copy(
                    src_ref=read_rows.at[source],
                    dst_ref=got.at[source],
                    send_sem=back_send.at[(head + HEADS - source) % HEADS],
                    recv_sem=back_recv.at[(head + HEADS - source) % HEADS],
                    device_id={"head": source},
                    device_id_type=MESH,
                ).wait_recv()

        rows = jnp.concatenate([got[there * 2], got[there * 2 + 1]], axis=1)
        depth = pl.multiple_of(there * 2 * HDIM, 2 * HDIM)
        total = total + dot(rows, out_w[pl.ds(depth, 2 * HDIM)])
    out_ref[...] = total.astype(BF16)
    for copy in sent:
        copy.wait_send()


def layer(*operands):
    smem = pl.BlockSpec(memory_space=pltpu.SMEM)
    vmem = pl.BlockSpec(memory_space=pltpu.VMEM)
    hbm = pl.BlockSpec(memory_space=pl.ANY)
    dma = pltpu.SemaphoreType.DMA
    return pl.pallas_call(
        layer_kernel,
        name="layer",
        out_shape=jax.ShapeDtypeStruct((TOK, D), BF16),
        in_specs=[smem] * 6 + [vmem] * 6 + [hbm] * 4,
        out_specs=vmem,
        scratch_shapes=[
            pltpu.VMEM((HEADS, TOK, WIDE), BF16),
            pltpu.VMEM((HDIM, 2 * HDIM), BF16),
            pltpu.VMEM((POOL_DEV, PAGE, HDIM), BF16),
            pltpu.VMEM((POOL_DEV, PAGE, HDIM), BF16),
            pltpu.VMEM((HEADS, D, PART), BF16),
            pltpu.VMEM((HDIM, 2 * HDIM), F32),
            pltpu.VMEM((NY, NZ, ROWS_A, 2 * HDIM), BF16),
            pltpu.VMEM((NY, NZ, ROWS_B, 2 * HDIM), BF16),
            pltpu.VMEM((NY, ROWS_A, 2 * HDIM), BF16),
            pltpu.VMEM((NZ, ROWS_B, 2 * HDIM), BF16),
            pltpu.VMEM((2, 4, NY, ROWS_A, 2 * HDIM), BF16),
            pltpu.VMEM((2, 2, NZ, ROWS_B, 2 * HDIM), BF16),
            pltpu.VMEM((2, 2, 1, ROWS_A, 2 * HDIM), BF16),
            pltpu.VMEM((2, 4, 1, ROWS_B, 2 * HDIM), BF16),
            pltpu.VMEM((TAIL, D), BF16),
            pltpu.VMEM((TAIL + TOK, D), BF16),
            pltpu.VMEM((2, TAIL + TOK, PART), F32),
            pltpu.VMEM((HEADS, TOK, WIDE), BF16),
            dma((8,)),
            dma((HEADS,)),
            dma((len(IDS),)),
            dma((len(IDS),)),
            dma((HEADS,)),
            dma((HEADS,)),
            pltpu.VMEM((HDIM, NEW), BF16),
            pltpu.VMEM((NEW, NEW), F32),
            pltpu.VMEM((8, NEW), F32),
            pltpu.VMEM((NEW, HDIM), F32),
            pltpu.VMEM((NEW, HDIM), F32),
            pltpu.VMEM((NEW, HDIM), F32),
            pltpu.VMEM((NEW, HDIM), F32),
            pltpu.VMEM((HEADS * HDIM, D), BF16),
            pltpu.VMEM((HEADS, TOK, HDIM), BF16),
            pltpu.VMEM((HEADS, TOK, HDIM), BF16),
            dma,
            dma((HEADS,)),
            dma((HEADS,)),
        ],
        compiler_params=pltpu.CompilerParams(
            collective_id=0, has_side_effects=True, vmem_limit_bytes=60 * 2**20
        ),
    )(*operands)


def shards(
    tokens,
    norm_gain,
    w_qkv,
    w_gates,
    conv_weight,
    conv_state,
    decay_rate,
    ridge,
    w_out,
    cache_keys,
    cache_values,
    page_table,
    cache_lengths,
    group_prompt,
    prompt_state,
):
    local = page_table - lax.axis_index("grp") * POOL_DEV
    here = (local >= 0) & (local < POOL_DEV)
    code = jnp.arange(page_table.shape[1])[None, :] * POOL_DEV + local
    low = jnp.min(jnp.where(here, code, 1 << 20), axis=1)
    high = jnp.max(jnp.where(here, code, -1), axis=1)
    return layer(
        low,
        high,
        cache_lengths,
        group_prompt,
        decay_rate,
        ridge,
        tokens,
        norm_gain.reshape(1, D),
        w_gates.T,
        conv_weight,
        conv_state,
        prompt_state,
        w_qkv,
        cache_keys.reshape(POOL_DEV, PAGE, HDIM),
        cache_values.reshape(POOL_DEV, PAGE, HDIM),
        w_out,
    )


def solution(mesh):
    placed = (
        P(("grp", "head"), None),
        P(),
        P(),
        P(),
        P(),
        P("grp", None, None),
        P(),
        P("head"),
        P(),
        P("grp", None, "head", None),
        P("grp", None, "head", None),
        P(),
        P(),
        P(),
        P("grp", "head", None, None, None),
    )
    return jax.shard_map(
        shards, mesh=mesh, in_specs=placed, out_specs=P(("grp", "head"), None), check_vma=False
    )
```

time: 59.5 us -> 52.1 us (0.88)
  Pallas kernels: 54.5 us -> 48.4 us
  local copies, waits for them, and re-layouts: 2.6 us -> 1.57 us
    pallas_call x3 -> x1, Pallas kernels: 54.5 us -> 48.4 us  [layer(): pl.pallas_call(layer_kernel, name='layer', out_shape=jax.ShapeDtypeStruct...]
    unnamed x9 -> x1, local copies, waits for them, and re-layouts: 2.6 us -> 1.57 us
where the time goes in v2:
time: 52.1 us; the launch traced here: 51.9 us
  Pallas kernels  48.4 us (93%)
  local copies, waits for them, and re-layouts  1.57 us (3%)
  other arithmetic  1.35 us (3%)
  between operations  0.67 us (1%)
    pallas_call x1, Pallas kernels, layer(): pl.pallas_call(layer_kernel, name='layer', out_shape=jax.ShapeDtypeStruct...  48.4 us
    unnamed x1, local copies, waits for them, and re-layouts  1.57 us
    reduce_max x1, other arithmetic, shards(): high = jnp.max(jnp.where(here, code, -1), axis=1)  1.35 us

profile of v2, /device:TPU:1, one launch (start us, length us, event | category | flops | bytes accessed | tf_op | source)
XLA Modules:
  0.0 51.9 jit_solution(14661468725067857903)
XLA Ops:
  0.7 1.4 %select_reduce_fusion = (s32[32]{0:T(128)}, s32[32]{0:T(128)}) fusion(s32[32,64]{1,0:T(8,128)} %param.26, s32[64]{0:T(128)S(1)} %iota_multiply_fusion, s32[]{:T(128)S(6)} %mul.14), kind=kLoop, calls=%fused_computation | loop fusion | flops 18368 | bytes 8708 | tf_op jit(solution)/shard_map/reduce_max | solution.py:608
  2.0 48.4 %layer.1 = bf16[64,1024]{1,0:T(8,128)(2,1)} custom-call(s32[32]{0:T(128)} %get-tuple-element.6.low_ref, s32[32]{0:T(128)} %get-tuple-element.5.high_ref, s32[32]{0:T(128)} %length_ref.1, s32[32]{0:T(128)} %prompt_of_ref.1, f32[8]{0:T(128)} %decay_ref.1, f32[1]{0:T(128)S(6)} %copy.17.ridge_ref, bf16[64,1024]{1,0:T(8,128)(2,1)} %tokens_ref.1, ...), custom_call_target="tpu_custom_call" | custom-call | tf_op jit(solution)/shard_map/layer/pallas_call | solution.py:536
  50.4 1.6 %copy.18 = bf16[64,1024]{1,0:T(8,128)(2,1)} copy(bf16[64,1024]{1,0:T(8,128)(2,1)} %layer.1) | data formatting | bytes 262144
  (1 shorter events, 0.0 us)

commit v3 on v2

--- a/solution.py
+++ b/solution.py
@@ -13,6 +13,7 @@
 CG_STEPS = 8
 PAGE = 128
 POOL_DEV = 64
+REQS = 32
 NY = 4
 NZ = 8
 TOK = NEW // HEADS
@@ -134,8 +135,6 @@
 
 
 def layer_kernel(
-    low_ref,
-    high_ref,
     length_ref,
     prompt_of_ref,
     decay_ref,
@@ -146,6 +145,7 @@
     conv_ref,
     stored_ref,
     prompt_ref,
+    table_ref,
     w_hbm,
     keys_hbm,
     values_hbm,
@@ -188,6 +188,9 @@
     out_sem,
     back_send,
     back_recv,
+    code_rows,
+    codes,
+    code_sem,
 ):
     grp = lax.axis_index("grp")
     head = lax.axis_index("head")
@@ -201,6 +204,15 @@
 
     def at_head(dh):
         return {"head": (head + dh) % HEADS}
+
+    local = table_ref[...] - grp * POOL_DEV
+    here = (local >= 0) & (local < POOL_DEV)
+    code = lax.broadcasted_iota(jnp.int32, local.shape, 1) * POOL_DEV + local
+    low = jnp.min(jnp.where(here, code, 1 << 20), axis=1, keepdims=True)
+    high = jnp.max(jnp.where(here, code, -1), axis=1, keepdims=True)
+    side = lax.broadcasted_iota(jnp.int32, code_rows.shape, 1)
+    code_rows[...] = jnp.where(side == 0, low, high)
+    code_load = pltpu.make_async_copy(code_rows, codes, code_sem)
 
     loads = []
     pieces = 4
@@ -231,6 +243,7 @@
     for peer in peers:
         pl.semaphore_signal(barrier, inc=1, device_id=peer, device_id_type=MESH)
 
+    code_load.start()
     own_prompt[:, :HDIM] = prompt_ref[0, 0, 0].T
     own_prompt[:, HDIM:] = prompt_ref[0, 0, 1].T
     normed[TAIL:] = rms_rows(tokens_ref[...], gain_ref[...])
@@ -274,6 +287,7 @@
         flying[kind, way, far, piece].wait_recv()
         return landing(kind, way, far, piece)[...].astype(F32)
 
+    code_load.wait()
     for copy in loads:
         copy.wait()
 
@@ -289,8 +303,8 @@
     def term(dy, dz):
         request = (y + dy) % NY * NZ + (z + dz) % NZ
         length = length_ref[request]
-        k0, kv0 = page_pair(low_ref[request], length)
-        k1, kv1 = page_pair(high_ref[request], length)
+        k0, kv0 = page_pair(codes[request, 0], length)
+        k1, kv1 = page_pair(codes[request, 1], length)
         total = lax.dot_general(
             jnp.concatenate([k0, k1], axis=0),
             jnp.concatenate([kv0, kv1], axis=0),
@@ -491,7 +505,7 @@
     for b in range(blocks):
         query = residue[b * HDIM : (b + 1) * HDIM]
         norms.append(jnp.sum(query * query, axis=-1, keepdims=True))
-    lax.fori_loop(0, CG_STEPS, step, tuple(norms))
+    lax.fori_loop(0, CG_STEPS, step, tuple(norms), unroll=True)
     for b in range(blocks):
         rows = slice(b * HDIM, (b + 1) * HDIM)
         result = read(b, solved[rows], start[:, HDIM:], part_of(2 * HDIM)).astype(BF16)
@@ -537,7 +551,7 @@
         layer_kernel,
         name="layer",
         out_shape=jax.ShapeDtypeStruct((TOK, D), BF16),
-        in_specs=[smem] * 6 + [vmem] * 6 + [hbm] * 4,
+        in_specs=[smem] * 4 + [vmem] * 7 + [hbm] * 4,
         out_specs=vmem,
         scratch_shapes=[
             pltpu.VMEM((HEADS, TOK, WIDE), BF16),
@@ -577,6 +591,9 @@
             dma,
             dma((HEADS,)),
             dma((HEADS,)),
+            pltpu.VMEM((REQS, HDIM), jnp.int32),
+            pltpu.SMEM((REQS, HDIM), jnp.int32),
+            dma,
         ],
         compiler_params=pltpu.CompilerParams(
             collective_id=0, has_side_effects=True, vmem_limit_bytes=60 * 2**20
@@ -601,14 +618,7 @@
     group_prompt,
     prompt_state,
 ):
-    local = page_table - lax.axis_index("grp") * POOL_DEV
-    here = (local >= 0) & (local < POOL_DEV)
-    code = jnp.arange(page_table.shape[1])[None, :] * POOL_DEV + local
-    low = jnp.min(jnp.where(here, code, 1 << 20), axis=1)
-    high = jnp.max(jnp.where(here, code, -1), axis=1)
     return layer(
-        low,
-        high,
         cache_lengths,
         group_prompt,
         decay_rate,
@@ -619,6 +629,7 @@
         conv_weight,
         conv_state,
         prompt_state,
+        page_table,
         w_qkv,
         cache_keys.reshape(POOL_DEV, PAGE, HDIM),
         cache_values.reshape(POOL_DEV, PAGE, HDIM),

time: 52.1 us -> 48.7 us (0.935)
  Pallas kernels: 48.4 us -> 46.3 us
  other arithmetic: 1.35 us -> 0 us
    pallas_call x1, Pallas kernels: 48.4 us -> 46.3 us  [layer(): pl.pallas_call(layer_kernel, name='layer', out_shape=jax.ShapeDtypeStruct...]
    reduce_max x1 -> x0, other arithmetic: 1.35 us -> none  [shards(): high = jnp.max(jnp.where(here, code, -1), axis=1)]
where the time goes in v3:
time: 48.7 us; the launch traced here: 48.6 us
  Pallas kernels  46.3 us (95%)
  local copies, waits for them, and re-layouts  1.57 us (3%)
  between operations  0.66 us (1%)
    pallas_call x1, Pallas kernels, layer(): pl.pallas_call(layer_kernel, name='layer', out_shape=jax.ShapeDtypeStruct...  46.3 us
    unnamed x1, local copies, waits for them, and re-layouts  1.57 us

profile of v3, /device:TPU:1, one launch (start us, length us, event | category | flops | bytes accessed | tf_op | source)
XLA Modules:
  0.0 48.6 jit_solution(10972135279318107214)
XLA Ops:
  0.7 46.3 %layer.1 = bf16[64,1024]{1,0:T(8,128)(2,1)} custom-call(s32[32]{0:T(128)} %length_ref.1, s32[32]{0:T(128)} %prompt_of_ref.1, f32[8]{0:T(128)} %decay_ref.1, f32[1]{0:T(128)S(6)} %copy.17.ridge_ref, bf16[64,1024]{1,0:T(8,128)(2,1)} %tokens_ref.1, f32[1,1024]{1,0:T(1,128)} %bitcast.7, bf16[16,1024]{1,0:T(8,128)(2,1)} %bitcast.6, f32[4,3072]{1,0:T(4,128)} %conv_ref.1, ...), custom_call_target="tpu_custom_call" | custom-call | tf_op jit(solution)/shard_map/layer/pallas_call | solution.py:550
  47.0 1.6 %copy.18 = bf16[64,1024]{1,0:T(8,128)(2,1)} copy(bf16[64,1024]{1,0:T(8,128)(2,1)} %layer.1) | data formatting | bytes 262144
